TPU v7x, 256 devices: a whole 4x4x8 slice. The times are simulated.
256 devices in a mesh: seq: 16 (over z, core), kvh: 8 (over y_hi, x), batch: 2 (over y_lo).
Axes of the slice: x: 4, y: 4 (y_hi: 2, y_lo: 2; y = y_hi * 2 + y_lo), z: 8, core: 2. Of those that a mesh axis runs over, the one named last changes fastest.
Arguments:
- query: bfloat16 [4096, 5120], P(('batch', 'seq'), 'kvh'), parts along dimension 0, may hold values from -33.3 to 33.3
- self_keys: bfloat16 [4096, 1024], P(('batch', 'seq'), 'kvh'), parts along dimension 0, may hold values from -6.4 to 6.4
- self_values: bfloat16 [4096, 1024], P(('batch', 'seq'), 'kvh'), parts along dimension 0, may hold values from -6 to 6
- cache_keys: bfloat16 [16384, 1024], P(('batch', 'seq'), 'kvh'), parts along dimension 0, may hold values from -6.375 to 6.375
- cache_values: bfloat16 [16384, 1024], P(('batch', 'seq'), 'kvh'), parts along dimension 0, may hold values from -6 to 6
- cache_pos: int32 [16384], P(('batch', 'seq')), parts along dimension 0, may hold values from 0 to 8191, each once
- d_out: bfloat16 [4096, 5120], P(('batch', 'seq'), 'kvh'), parts along dimension 0, may hold values from -6 to 6
Outputs:
- attended: bfloat16 [4096, 5120], P(('batch', 'seq'), 'kvh'), parts along dimension 0
- grad_query: bfloat16 [4096, 5120], P(('batch', 'seq'), 'kvh'), parts along dimension 0
- grad_keys: bfloat16 [4096, 1024], P(('batch', 'seq'), 'kvh'), parts along dimension 0
- grad_values: bfloat16 [4096, 1024], P(('batch', 'seq'), 'kvh'), parts along dimension 0
There are 2 independent parts, one for each index of `batch`. A program takes and returns all parts, laid end to end along the dimension named above; each array names one. Nothing has to cross between parts.
Inputs may be any that keep to these rules, and one draw needn't show every extreme that they name: `cache_pos`: each cache position appears once.
All inputs are finite; a program needn't handle non-finite values.
Results may differ from a plain program's by a relative error of at most 0.012.
The roundings to bfloat16 on the way count: a program that leaves them out, or rounds other values in their place, can miss the bound.
Values may be sent and summed in bfloat16 or wider, within the bound.
No kernel may reach another device: no remote copies, remote signals or barrier semaphores. Data moves between devices by JAX's collectives and lax.ppermute only.
A program may use at most 64 MiB of HBM per device.

v0:
```python
import jax
import jax.numpy as jnp
from jax import lax
from jax.sharding import PartitionSpec as P

HD = 128
GROUP = 5
WINDOW = 512


def shifted(block, axis, distance):
    devices = range(lax.axis_size(axis))
    route = [(i - distance, i) for i in devices if i - distance in devices]
    return lax.ppermute(block, axis, route)


def copy_for_each(value, axis):
    peers = lax.axis_size(axis)
    return lax.all_to_all(
        jnp.broadcast_to(value[None], (peers, *value.shape)), axis, 0, 0, tiled=True
    )


def laid_out(blocks, dim):
    blocks = jnp.moveaxis(blocks, 0, dim)
    shape = blocks.shape
    return blocks.reshape(*shape[:dim], shape[dim] * shape[dim + 1], *shape[dim + 2 :])


def gather_directly(value, axis, dim):
    blocks = copy_for_each(value, axis)
    return laid_out(blocks, dim)


def side_by_side(arrays, axis, dim, along):
    widths = [a.shape[along] for a in arrays]
    both = jnp.concatenate(arrays, axis=along)
    out = lax.all_gather(both, axis, axis=dim, tiled=True)
    return tuple(jnp.split(out, [sum(widths[:k]) for k in range(1, len(widths))], axis=along))


def cache_limit(anchor, rows_dev, start_pos):
    row_index = anchor * rows_dev + jnp.arange(rows_dev, dtype=jnp.int32)
    return start_pos + jnp.maximum(row_index - WINDOW + 1, 0)


def forward_piece(partial_value, queries, bound_pos, key_rows, values, positions, scaling, final):
    scores = (
        jnp.einsum("tgd,cd->gtc", queries, key_rows, preferred_element_type=jnp.float32) * scaling
    )
    visible = positions[None, :] < bound_pos[:, None]
    scores = jnp.where(visible[None], scores, -jnp.inf)
    if not final:
        row_max, row_sum = partial_value
        new_max = jnp.maximum(row_max, jnp.max(scores, axis=2))
        factor = jnp.exp(row_max - new_max)
        row_sum = row_sum * factor + jnp.sum(jnp.exp(scores - new_max[:, :, None]), axis=2)
        return (new_max, row_sum)
    summed, log_total = partial_value
    weights = jnp.exp(scores - log_total[:, :, None]).astype(jnp.bfloat16)
    summed = summed + jnp.einsum("gtc,cd->gtd", weights, values, preferred_element_type=jnp.float32)
    return (summed, log_total)


def backward_piece(
    grad_acc,
    queries,
    grads_out,
    log_total,
    delta_rows,
    bound_pos,
    key_rows,
    values,
    positions,
    scaling,
):
    scores = (
        jnp.einsum("tgd,cd->gtc", queries, key_rows, preferred_element_type=jnp.float32) * scaling
    )
    visible = positions[None, :] < bound_pos[:, None]
    scores = jnp.where(visible[None], scores, -jnp.inf)
    weights = jnp.exp(scores - log_total[:, :, None])
    grad_weights = jnp.einsum("tgd,cd->gtc", grads_out, values, preferred_element_type=jnp.float32)
    grad_scores = (weights * (grad_weights - delta_rows[:, :, None])).astype(jnp.bfloat16)
    return grad_acc + jnp.einsum(
        "gtc,cd->tgd", grad_scores, key_rows, preferred_element_type=jnp.float32
    )


def fetch_earlier(pair, distance):
    return shifted((pair[0], pair[1]), "seq", distance)


def return_grads(pair, distance):
    return (
        shifted(pair[0].astype(jnp.bfloat16), "seq", -distance).astype(jnp.float32),
        shifted(pair[1].astype(jnp.bfloat16), "seq", -distance).astype(jnp.float32),
    )


def local(query, self_keys, self_values, cache_keys, cache_values, cache_pos, d_out):
    rows_dev = query.shape[0]
    cache_dev = cache_keys.shape[0]
    cycle_size = lax.axis_size("seq")
    my_index = lax.axis_index("seq")
    start_pos = cache_dev * cycle_size - rows_dev * cycle_size
    scaling = HD ** (-0.5)
    queries = query.reshape(rows_dev, GROUP, HD)
    grads_out = d_out.reshape(rows_dev, GROUP, HD)
    rim_count = (WINDOW + rows_dev - 2) // rows_dev
    pair = (self_keys, self_values)
    earlier = [fetch_earlier(pair, distance) for distance in range(rim_count, 0, -1)]
    window_keys = jnp.concatenate([member[0] for member in earlier] + [self_keys], axis=0)
    window_values = jnp.concatenate([member[1] for member in earlier] + [self_values], axis=0)
    window_rows = window_keys.shape[0]
    key_index = (my_index - rim_count) * rows_dev + jnp.arange(window_rows, dtype=jnp.int32)
    query_index = my_index * rows_dev + jnp.arange(rows_dev, dtype=jnp.int32)
    visible = (
        (key_index[None, :] <= query_index[:, None])
        & (key_index[None, :] >= query_index[:, None] - WINDOW + 1)
        & (key_index[None, :] >= 0)
    )
    scores = (
        jnp.einsum("tgd,cd->gtc", queries, window_keys, preferred_element_type=jnp.float32)
        * scaling
    )
    scores = jnp.where(visible[None], scores, -jnp.inf)
    row_max = jnp.max(scores, axis=2)
    row_sum = jnp.sum(jnp.exp(scores - row_max[:, :, None]), axis=2)
    own_limit = cache_limit(my_index, rows_dev, start_pos)
    held_positions = gather_directly(cache_pos, "seq", 0)
    held_keys, held_values = side_by_side((cache_keys, cache_values), "seq", 0, 1)
    held_count = held_keys.shape[0] // cache_dev
    held_shards = (
        held_keys.reshape(held_count, cache_dev, HD),
        held_values.reshape(held_count, cache_dev, HD),
        held_positions.reshape(held_count, cache_dev),
    )

    def run_tour(partial_value, final):

        def held_forward(running, shard_data):
            return (
                forward_piece(
                    running,
                    queries,
                    own_limit,
                    shard_data[0],
                    shard_data[1],
                    shard_data[2],
                    scaling,
                    final,
                ),
                None,
            )

        result, unused = lax.scan(held_forward, partial_value, held_shards)
        return result

    row_max, row_sum = run_tour((row_max, row_sum), False)
    log_total = row_max + jnp.log(row_sum)
    back_weights = jnp.exp(scores - log_total[:, :, None])
    back_rounded = back_weights.astype(jnp.bfloat16)
    summed = jnp.einsum(
        "gtc,cd->gtd", back_rounded, window_values, preferred_element_type=jnp.float32
    )
    summed, unused_total = run_tour((summed, log_total), True)
    attended = jnp.transpose(summed, (1, 0, 2)).astype(jnp.bfloat16)
    delta_rows = jnp.sum(grads_out.astype(jnp.float32) * attended.astype(jnp.float32), axis=2).T
    grad_weights = jnp.einsum(
        "tgd,cd->gtc", grads_out, window_values, preferred_element_type=jnp.float32
    )
    grad_scores = (back_weights * (grad_weights - delta_rows[:, :, None])).astype(jnp.bfloat16)
    grad_acc = jnp.einsum(
        "gtc,cd->tgd", grad_scores, window_keys, preferred_element_type=jnp.float32
    )
    key_grads = jnp.einsum("gtc,tgd->cd", grad_scores, queries, preferred_element_type=jnp.float32)
    value_grads = jnp.einsum(
        "gtc,tgd->cd", back_rounded, grads_out, preferred_element_type=jnp.float32
    )

    def held_backward(running, shard_data):
        return (
            backward_piece(
                running,
                queries,
                grads_out,
                log_total,
                delta_rows,
                own_limit,
                shard_data[0],
                shard_data[1],
                shard_data[2],
                scaling,
            ),
            None,
        )

    grad_acc, unused = lax.scan(held_backward, grad_acc, held_shards)
    key_blocks = key_grads.reshape(rim_count + 1, rows_dev, HD)
    value_blocks = value_grads.reshape(rim_count + 1, rows_dev, HD)
    total_keys = key_blocks[rim_count]
    total_values = value_blocks[rim_count]
    for distance in range(1, rim_count + 1):
        returned = return_grads(
            (key_blocks[rim_count - distance], value_blocks[rim_count - distance]), distance
        )
        total_keys = total_keys + returned[0]
        total_values = total_values + returned[1]
    grad_query = (grad_acc * scaling).astype(jnp.bfloat16).reshape(rows_dev, GROUP * HD)
    grad_keys = (total_keys * scaling).astype(jnp.bfloat16)
    grad_values = total_values.astype(jnp.bfloat16)
    return (attended.reshape(rows_dev, GROUP * HD), grad_query, grad_keys, grad_values)


def solution(mesh):
    in_specs = (
        P(("batch", "seq"), "kvh"),
        P(("batch", "seq"), "kvh"),
        P(("batch", "seq"), "kvh"),
        P(("batch", "seq"), "kvh"),
        P(("batch", "seq"), "kvh"),
        P(("batch", "seq")),
        P(("batch", "seq"), "kvh"),
    )
    out_specs = (
        P(("batch", "seq"), "kvh"),
        P(("batch", "seq"), "kvh"),
        P(("batch", "seq"), "kvh"),
        P(("batch", "seq"), "kvh"),
    )
    return jax.shard_map(local, mesh=mesh, in_specs=in_specs, out_specs=out_specs, check_vma=False)
```

profile of v0, /device:TPU:194, one launch (start us, length us, event | category | flops | bytes accessed | tf_op | source)
XLA Modules:
  0.0 199.3 jit_solution(14942992339636723227)
XLA Ops:
  7.2 1.8 pad_maximum_fusion
  9.0 2.9 %collective-permute-start.2 = (bf16[128,128]{1,0:T(8,128)(2,1)}, bf16[128,128]{1,0:T(8,128)(2,1)S(1)}, u32[]{:S(2)}, u32[]{:S(2)}) collective-permute-start(bf16[128,128]{1,0:T(8,128)(2,1)} %param.14), channel_id=1, source_target_pairs={{0,32},{16,48},{32,64},{48,80},{64,96},{80,112},{96,128},{112,144}... | collective-permute-start | bytes 98312 | tf_op jit(solution)/shard_map/ppermute | solution.py:14
  12.0 1.9 collective-permute-start.1
  15.2 1.9 collective-permute-start.3
  18.4 9.4 %all-to-all-start = ((s32[16,1,512]{2,1,0:T(1,128)}), s32[16,1,512]{2,1,0:T(1,128)S(1)}, u32[]{:S(2)}, u32[]{:S(2)}) async-start(s32[16,1,512]{2,1,0:T(1,128)} %broadcast_in_dim.70), calls=%async_computation | async-start | bytes 65536 | tf_op jit(solution)/shard_map/all_to_all | solution.py:19
  27.8 2.5 %collective-permute-start.6 = (bf16[128,128]{1,0:T(8,128)(2,1)}, bf16[128,128]{1,0:T(8,128)(2,1)S(1)}, u32[]{:S(2)}, u32[]{:S(2)}) collective-permute-start(bf16[128,128]{1,0:T(8,128)(2,1)} %param.15), channel_id=1, source_target_pairs={{0,32},{16,48},{32,64},{48,80},{64,96},{80,112},{96,128},{112,144}... | collective-permute-start | bytes 98312 | tf_op jit(solution)/shard_map/ppermute | solution.py:14
  32.2 1.9 collective-permute-start.5
  35.5 1.9 collective-permute-start.7
  37.5 4.4 %collective-permute-done.4 = bf16[128,128]{1,0:T(8,128)(2,1)S(1)} collective-permute-done((bf16[128,128]{1,0:T(8,128)(2,1)S(1)}, bf16[128,128]{1,0:T(8,128)(2,1)S(1)}, u32[]{:S(2)}, u32[]{:S(2)}) %collective-permute-start.4) | collective-permute-done | bytes 32800 | tf_op jit(solution)/shard_map/ppermute | solution.py:14
  42.7 10.1 %all-gather.2.cloned.1.call-done = bf16[8192,256]{1,0:T(8,128)(2,1)} async-done(((bf16[512,256]{1,0:T(8,128)(2,1)}), bf16[8192,256]{1,0:T(8,128)(2,1)}) %all-gather.2.cloned.1.call-update) | async-done | bytes 4194320 | tf_op jit(solution)/shard_map/all_gather | solution.py:38
  52.8 4.5 %fusion.74 = (bf16[8192,128]{1,0:T(8,128)(2,1)}, bf16[8192,128]{1,0:T(8,128)(2,1)}) fusion(bf16[8192,256]{1,0:T(8,128)(2,1)} %all-gather.2.cloned.1.call-done), kind=kLoop, calls=%fused_computation.107 | loop fusion | bytes 8388608 | tf_op jit(solution)/shard_map/split | solution.py:39
  57.3 26.9 %while.35 = (s32[]{:T(128)}, f32[5,128]{1,0:T(8,128)S(1)}, f32[5,128]{1,0:T(8,128)S(1)}, s32[16,512]{1,0:T(8,128)S(1)}, bf16[16,512,128]{2,1,0:T(8,128)(2,1)}, /...) while((s32[]{:T(128)}, f32[5,128]{1,0:T(8,128)S(1)}, f32[5,128]{1,0:T(8,128)S(1)}, ...), condition=%wide.region_5.6_spmd.clone, body=%wide.region_2.5_spmd.clone.sunk | while | flops 85591808 | bytes 3087977 | solution.py:157
  85.8 29.5 %while.36 = (s32[]{:T(128)}, f32[5,128,128]{2,1,0:T(8,128)S(1)}, s32[16,512]{1,0:T(8,128)S(1)}, bf16[16,512,128]{2,1,0:T(8,128)(2,1)}, bf16[128,5,128]{2,0,1:T(8...) while((s32[]{:T(128)}, f32[5,128,128]{2,1,0:T(8,128)S(1)}, ...), condition=%wide.region_7.8_spmd.clone, body=%wide.region_6.7_spmd.clone.sunk | while | flops 169230848 | bytes 1223277 | solution.py:157
  86.0 1.7 fusion.108
  87.8 1.7 fusion.108
  89.7 1.7 fusion.108
  91.5 1.6 fusion.108
  93.4 1.6 fusion.108
  95.2 1.6 fusion.108
  97.0 1.6 fusion.108
  98.9 1.6 fusion.108
  100.7 1.6 fusion.108
  102.6 1.6 fusion.108
  104.4 1.6 fusion.108
  106.3 1.6 fusion.108
  108.1 1.6 fusion.108
  110.0 1.6 fusion.108
  111.8 1.6 fusion.108
  113.6 1.6 fusion.108
  116.7 2.6 %collective-permute-start.12 = (bf16[128,128]{1,0:T(8,128)(2,1)S(1)}, bf16[128,128]{1,0:T(8,128)(2,1)S(1)}, u32[]{:S(2)}, u32[]{:S(2)}) collective-permute-start(bf16[128,128]{1,0:T(8,128)(2,1)S(1)} %get-tuple-element.326), channel_id=1, source_target_pairs={{16,0},{32,16},{48,32},{64,48},{80,64},{96,80},{112,96},{128,112},... | collective-permute-start | bytes 98312 | tf_op jit(solution)/shard_map/ppermute | solution.py:14
  119.3 4.6 %collective-permute-start.15 = (bf16[128,128]{1,0:T(8,128)(2,1)S(1)}, bf16[128,128]{1,0:T(8,128)(2,1)S(1)}, u32[]{:S(2)}, u32[]{:S(2)}) collective-permute-start(bf16[128,128]{1,0:T(8,128)(2,1)S(1)} %get-tuple-element.327), channel_id=1, source_target_pairs={{64,0},{80,16},{96,32},{112,48},{128,64},{144,80},{160,96},{176,11... | collective-permute-start | bytes 98312 | tf_op jit(solution)/shard_map/ppermute | solution.py:14
  123.9 2.5 %collective-permute-start.14 = (bf16[128,128]{1,0:T(8,128)(2,1)S(1)}, bf16[128,128]{1,0:T(8,128)(2,1)S(1)}, u32[]{:S(2)}, u32[]{:S(2)}) collective-permute-start(bf16[128,128]{1,0:T(8,128)(2,1)S(1)} %get-tuple-element.328), channel_id=1, source_target_pairs={{48,0},{64,16},{80,32},{96,48},{112,64},{128,80},{144,96},{160,112... | collective-permute-start | bytes 98312 | tf_op jit(solution)/shard_map/ppermute | solution.py:14
  126.4 2.5 %collective-permute-start.13 = (bf16[128,128]{1,0:T(8,128)(2,1)S(1)}, bf16[128,128]{1,0:T(8,128)(2,1)S(1)}, u32[]{:S(2)}, u32[]{:S(2)}) collective-permute-start(bf16[128,128]{1,0:T(8,128)(2,1)S(1)} %get-tuple-element.329), channel_id=1, source_target_pairs={{32,0},{48,16},{64,32},{80,48},{96,64},{112,80},{128,96},{144,112}... | collective-permute-start | bytes 98312 | tf_op jit(solution)/shard_map/ppermute | solution.py:14
  128.9 48.6 %while.37 = (s32[]{:T(128)}, f32[128,5,128]{0,2,1:T(8,128)S(1)}, bf16[16,512,128]{2,1,0:T(8,128)(2,1)}, s32[16,512]{1,0:T(8,128)S(1)}, bf16[128,5,128]{2,0,1:T(8...) while((s32[]{:T(128)}, f32[128,5,128]{0,2,1:T(8,128)S(1)}, ...), condition=%wide.region_10.11_spmd.clone, body=%wide.region_9.10_spmd.clone.sunk | while | flops 253772288 | bytes 4142209 | solution.py:199
  136.5 1.5 fusion.115
  139.6 1.5 fusion.115
  142.6 1.5 fusion.115
  145.6 1.5 fusion.115
  148.7 1.5 fusion.115
  151.7 1.5 fusion.115
  154.8 1.5 fusion.115
  157.8 1.5 fusion.115
  160.8 1.5 fusion.115
  179.3 2.7 %collective-permute-start.8 = (bf16[128,128]{1,0:T(8,128)(2,1)S(1)}, bf16[128,128]{1,0:T(8,128)(2,1)S(1)}, u32[]{:S(2)}, u32[]{:S(2)}) collective-permute-start(bf16[128,128]{1,0:T(8,128)(2,1)S(1)} %get-tuple-element.330), channel_id=1, source_target_pairs={{16,0},{32,16},{48,32},{64,48},{80,64},{96,80},{112,96},{128,112},... | collective-permute-start | bytes 98312 | tf_op jit(solution)/shard_map/ppermute | solution.py:14
  182.0 1.9 collective-permute-start.11
  183.9 2.0 %collective-permute-start.10 = (bf16[128,128]{1,0:T(8,128)(2,1)S(1)}, bf16[128,128]{1,0:T(8,128)(2,1)S(1)}, u32[]{:S(2)}, u32[]{:S(2)}) collective-permute-start(bf16[128,128]{1,0:T(8,128)(2,1)S(1)} %get-tuple-element.332), channel_id=1, source_target_pairs={{48,0},{64,16},{80,32},{96,48},{112,64},{128,80},{144,96},{160,112... | collective-permute-start | bytes 98312 | tf_op jit(solution)/shard_map/ppermute | solution.py:14
  186.0 2.1 %collective-permute-start.9 = (bf16[128,128]{1,0:T(8,128)(2,1)S(1)}, bf16[128,128]{1,0:T(8,128)(2,1)S(1)}, u32[]{:S(2)}, u32[]{:S(2)}) collective-permute-start(bf16[128,128]{1,0:T(8,128)(2,1)S(1)} %get-tuple-element.333), channel_id=1, source_target_pairs={{32,0},{48,16},{64,32},{80,48},{96,64},{112,80},{128,96},{144,112}... | collective-permute-start | bytes 98312 | tf_op jit(solution)/shard_map/ppermute | solution.py:14
  189.6 2.2 %collective-permute-done.9 = bf16[128,128]{1,0:T(8,128)(2,1)S(1)} collective-permute-done((bf16[128,128]{1,0:T(8,128)(2,1)S(1)}, bf16[128,128]{1,0:T(8,128)(2,1)S(1)}, u32[]{:S(2)}, u32[]{:S(2)}) %collective-permute-start.9) | collective-permute-done | bytes 32800 | tf_op jit(solution)/shard_map/ppermute | solution.py:14
  (309 shorter events, 76.0 us)
Async XLA Ops:
  7.2 30.3 %copy-start.1 = (bf16[128,128]{1,0:T(8,128)(2,1)S(1)}, bf16[128,128]{1,0:T(8,128)(2,1)}, u32[]{:S(2)}) copy-start(bf16[128,128]{1,0:T(8,128)(2,1)} %param.14) | copy-start | bytes 98308
  7.2 25.0 %copy-start.2 = (bf16[128,128]{1,0:T(8,128)(2,1)S(1)}, bf16[128,128]{1,0:T(8,128)(2,1)}, u32[]{:S(2)}) copy-start(bf16[128,128]{1,0:T(8,128)(2,1)} %param.15) | copy-start | bytes 98308
  7.2 24.7 %copy-start = (bf16[128,640]{1,0:T(8,128)(2,1)S(1)}, bf16[128,640]{1,0:T(8,128)(2,1)}, u32[]{:S(2)}) copy-start(bf16[128,640]{1,0:T(8,128)(2,1)} %param.19) | copy-start | bytes 491524
  7.2 45.6 %all-gather.2.cloned.1.call-start = ((), (), s32[]{:S(2)}) async-start(), calls=%async_computation.1 | async-start | bytes 4456448 | tf_op jit(solution)/shard_map/all_gather | solution.py:38
  9.0 26.5 %collective-permute-start.2 = (bf16[128,128]{1,0:T(8,128)(2,1)}, bf16[128,128]{1,0:T(8,128)(2,1)S(1)}, u32[]{:S(2)}, u32[]{:S(2)}) collective-permute-start(bf16[128,128]{1,0:T(8,128)(2,1)} %param.14), channel_id=1, source_target_pairs={{0,32},{16,48},{32,64},{48,80},{64,96},{80,112},{96,128},{112,144}... | collective-permute-start | bytes 98312 | tf_op jit(solution)/shard_map/ppermute | solution.py:14
  12.0 22.2 %collective-permute-start.1 = (bf16[128,128]{1,0:T(8,128)(2,1)}, bf16[128,128]{1,0:T(8,128)(2,1)S(1)}, u32[]{:S(2)}, u32[]{:S(2)}) collective-permute-start(bf16[128,128]{1,0:T(8,128)(2,1)} %param.14), channel_id=1, source_target_pairs={{0,48},{16,64},{32,80},{48,96},{64,112},{80,128},{96,144},{112,160... | collective-permute-start | bytes 98312 | tf_op jit(solution)/shard_map/ppermute | solution.py:14
  13.9 18.3 %collective-permute-start = (bf16[128,128]{1,0:T(8,128)(2,1)}, bf16[128,128]{1,0:T(8,128)(2,1)S(1)}, u32[]{:S(2)}, u32[]{:S(2)}) collective-permute-start(bf16[128,128]{1,0:T(8,128)(2,1)} %param.14), channel_id=1, source_target_pairs={{0,64},{16,80},{32,96},{48,112},{64,128},{80,144},{96,160},{112,17... | collective-permute-start | bytes 98312 | tf_op jit(solution)/shard_map/ppermute | solution.py:14
  15.2 22.2 %collective-permute-start.3 = (bf16[128,128]{1,0:T(8,128)(2,1)}, bf16[128,128]{1,0:T(8,128)(2,1)S(1)}, u32[]{:S(2)}, u32[]{:S(2)}) collective-permute-start(bf16[128,128]{1,0:T(8,128)(2,1)} %param.14), channel_id=1, source_target_pairs={{0,16},{16,32},{32,48},{48,64},{64,80},{80,96},{96,112},{112,128},... | collective-permute-start | bytes 98312 | tf_op jit(solution)/shard_map/ppermute | solution.py:14
  18.4 24.3 %all-to-all-start = ((s32[16,1,512]{2,1,0:T(1,128)}), s32[16,1,512]{2,1,0:T(1,128)S(1)}, u32[]{:S(2)}, u32[]{:S(2)}) async-start(s32[16,1,512]{2,1,0:T(1,128)} %broadcast_in_dim.70), calls=%async_computation | async-start | bytes 65536 | tf_op jit(solution)/shard_map/all_to_all | solution.py:19
  27.8 14.1 %collective-permute-start.6 = (bf16[128,128]{1,0:T(8,128)(2,1)}, bf16[128,128]{1,0:T(8,128)(2,1)S(1)}, u32[]{:S(2)}, u32[]{:S(2)}) collective-permute-start(bf16[128,128]{1,0:T(8,128)(2,1)} %param.15), channel_id=1, source_target_pairs={{0,32},{16,48},{32,64},{48,80},{64,96},{80,112},{96,128},{112,144}... | collective-permute-start | bytes 98312 | tf_op jit(solution)/shard_map/ppermute | solution.py:14
  32.2 9.7 %collective-permute-start.5 = (bf16[128,128]{1,0:T(8,128)(2,1)S(1)}, bf16[128,128]{1,0:T(8,128)(2,1)S(1)}, u32[]{:S(2)}, u32[]{:S(2)}) collective-permute-start(bf16[128,128]{1,0:T(8,128)(2,1)S(1)} %copy-done.2), channel_id=1, source_target_pairs={{0,48},{16,64},{32,80},{48,96},{64,112},{80,128},{96,144},{112,160... | collective-permute-start | bytes 98312 | tf_op jit(solution)/shard_map/ppermute | solution.py:14
  34.2 7.7 %collective-permute-start.4 = (bf16[128,128]{1,0:T(8,128)(2,1)S(1)}, bf16[128,128]{1,0:T(8,128)(2,1)S(1)}, u32[]{:S(2)}, u32[]{:S(2)}) collective-permute-start(bf16[128,128]{1,0:T(8,128)(2,1)S(1)} %copy-done.2), channel_id=1, source_target_pairs={{0,64},{16,80},{32,96},{48,112},{64,128},{80,144},{96,160},{112,17... | collective-permute-start | bytes 98312 | tf_op jit(solution)/shard_map/ppermute | solution.py:14
  35.5 6.6 %collective-permute-start.7 = (bf16[128,128]{1,0:T(8,128)(2,1)S(1)}, bf16[128,128]{1,0:T(8,128)(2,1)S(1)}, u32[]{:S(2)}, u32[]{:S(2)}) collective-permute-start(bf16[128,128]{1,0:T(8,128)(2,1)S(1)} %copy-done.2), channel_id=1, source_target_pairs={{0,16},{16,32},{32,48},{48,64},{64,80},{80,96},{96,112},{112,128},... | collective-permute-start | bytes 98312 | tf_op jit(solution)/shard_map/ppermute | solution.py:14
  116.7 65.3 %collective-permute-start.12 = (bf16[128,128]{1,0:T(8,128)(2,1)S(1)}, bf16[128,128]{1,0:T(8,128)(2,1)S(1)}, u32[]{:S(2)}, u32[]{:S(2)}) collective-permute-start(bf16[128,128]{1,0:T(8,128)(2,1)S(1)} %get-tuple-element.326), channel_id=1, source_target_pairs={{16,0},{32,16},{48,32},{64,48},{80,64},{96,80},{112,96},{128,112},... | collective-permute-start | bytes 98312 | tf_op jit(solution)/shard_map/ppermute | solution.py:14
  119.3 64.6 %collective-permute-start.15 = (bf16[128,128]{1,0:T(8,128)(2,1)S(1)}, bf16[128,128]{1,0:T(8,128)(2,1)S(1)}, u32[]{:S(2)}, u32[]{:S(2)}) collective-permute-start(bf16[128,128]{1,0:T(8,128)(2,1)S(1)} %get-tuple-element.327), channel_id=1, source_target_pairs={{64,0},{80,16},{96,32},{112,48},{128,64},{144,80},{160,96},{176,11... | collective-permute-start | bytes 98312 | tf_op jit(solution)/shard_map/ppermute | solution.py:14
  123.9 62.1 %collective-permute-start.14 = (bf16[128,128]{1,0:T(8,128)(2,1)S(1)}, bf16[128,128]{1,0:T(8,128)(2,1)S(1)}, u32[]{:S(2)}, u32[]{:S(2)}) collective-permute-start(bf16[128,128]{1,0:T(8,128)(2,1)S(1)} %get-tuple-element.328), channel_id=1, source_target_pairs={{48,0},{64,16},{80,32},{96,48},{112,64},{128,80},{144,96},{160,112... | collective-permute-start | bytes 98312 | tf_op jit(solution)/shard_map/ppermute | solution.py:14
  126.4 61.6 %collective-permute-start.13 = (bf16[128,128]{1,0:T(8,128)(2,1)S(1)}, bf16[128,128]{1,0:T(8,128)(2,1)S(1)}, u32[]{:S(2)}, u32[]{:S(2)}) collective-permute-start(bf16[128,128]{1,0:T(8,128)(2,1)S(1)} %get-tuple-element.329), channel_id=1, source_target_pairs={{32,0},{48,16},{64,32},{80,48},{96,64},{112,80},{128,96},{144,112}... | collective-permute-start | bytes 98312 | tf_op jit(solution)/shard_map/ppermute | solution.py:14
  179.3 10.3 %collective-permute-start.8 = (bf16[128,128]{1,0:T(8,128)(2,1)S(1)}, bf16[128,128]{1,0:T(8,128)(2,1)S(1)}, u32[]{:S(2)}, u32[]{:S(2)}) collective-permute-start(bf16[128,128]{1,0:T(8,128)(2,1)S(1)} %get-tuple-element.330), channel_id=1, source_target_pairs={{16,0},{32,16},{48,32},{64,48},{80,64},{96,80},{112,96},{128,112},... | collective-permute-start | bytes 98312 | tf_op jit(solution)/shard_map/ppermute | solution.py:14
  182.0 7.6 %collective-permute-start.11 = (bf16[128,128]{1,0:T(8,128)(2,1)S(1)}, bf16[128,128]{1,0:T(8,128)(2,1)S(1)}, u32[]{:S(2)}, u32[]{:S(2)}) collective-permute-start(bf16[128,128]{1,0:T(8,128)(2,1)S(1)} %get-tuple-element.331), channel_id=1, source_target_pairs={{64,0},{80,16},{96,32},{112,48},{128,64},{144,80},{160,96},{176,11... | collective-permute-start | bytes 98312 | tf_op jit(solution)/shard_map/ppermute | solution.py:14
  183.9 5.6 %collective-permute-start.10 = (bf16[128,128]{1,0:T(8,128)(2,1)S(1)}, bf16[128,128]{1,0:T(8,128)(2,1)S(1)}, u32[]{:S(2)}, u32[]{:S(2)}) collective-permute-start(bf16[128,128]{1,0:T(8,128)(2,1)S(1)} %get-tuple-element.332), channel_id=1, source_target_pairs={{48,0},{64,16},{80,32},{96,48},{112,64},{128,80},{144,96},{160,112... | collective-permute-start | bytes 98312 | tf_op jit(solution)/shard_map/ppermute | solution.py:14
  186.0 5.8 %collective-permute-start.9 = (bf16[128,128]{1,0:T(8,128)(2,1)S(1)}, bf16[128,128]{1,0:T(8,128)(2,1)S(1)}, u32[]{:S(2)}, u32[]{:S(2)}) collective-permute-start(bf16[128,128]{1,0:T(8,128)(2,1)S(1)} %get-tuple-element.333), channel_id=1, source_target_pairs={{32,0},{48,16},{64,32},{80,48},{96,64},{112,80},{128,96},{144,112}... | collective-permute-start | bytes 98312 | tf_op jit(solution)/shard_map/ppermute | solution.py:14
Sparse Core Ops, SparseCore 0:
  9.8 42.9 all-gather.1
where the time goes:
time: 201 us; the launch traced here: 199 us
  matrix products  94.9 us (47%)
  starting transfers between devices  46 us (23%)
  waiting for transfers between devices  16.8 us (8%)
  other arithmetic  14.5 us (7%)
  between operations  14.5 us (7%)
  local copies, waits for them, and re-layouts  9.95 us (5%)
  loops' own time  2.63 us (1%)
    ppermute x16, starting transfers between devices, shifted(): return lax.ppermute(block, axis, route)  36.6 us
    dot_general x16, matrix products, forward_piece(): jnp.einsum('gtc,cd->gtd', weights, values, preferred_element_type=jnp.flo...  26.4 us
    dot_general x16, matrix products, backward_piece(): jnp.einsum('gtc,cd->tgd', grad_scores, key_rows, preferred_element_type=j...  24.1 us
    dot_general x16, matrix products, backward_piece(): jnp.einsum('tgd,cd->gtc', queries, key_rows, preferred_element_type=jnp.f...  21.3 us
    dot_general x16, matrix products, forward_piece(): jnp.einsum('tgd,cd->gtc', queries, key_rows, preferred_element_type=jnp.f...  20.1 us
    all_gather x1, waiting for transfers between devices, side_by_side(): out = lax.all_gather(both, axis, axis=dim, tiled=True)  10.1 us
    all_to_all x1, starting transfers between devices, copy_for_each(): lax.all_to_all(jnp.broadcast_to(value[None], (peers, *value.shape)), axis...  9.37 us
    ppermute x16, waiting for transfers between devices, shifted(): return lax.ppermute(block, axis, route)  6.76 us
  transfers between devices with their start and end apart: 18, of which 4 were waited for; matrix products, arithmetic and copies ran while one was open for 28% of the time, Pallas kernels for 0%

commit v1 on v0

v1 whole, which is shorter than its diff:
```python
import functools

import jax
import jax.numpy as jnp
from jax import lax
from jax.experimental import pallas as pl
from jax.experimental.pallas import tpu as pltpu
from jax.sharding import PartitionSpec as P

HD = 128
GROUP = 5
WINDOW = 512
LANES = 128
NEG = -1e30
SCALE = HD**-0.5
EXP2_SCALE = SCALE * 1.4426950408889634
POS_BASE = 128
POS_ROWS = 16


def nt(a, b):
    return lax.dot_general(a, b, (((1,), (1,)), ((), ())), preferred_element_type=jnp.float32)


def nn(a, b):
    return lax.dot_general(a, b, (((1,), (0,)), ((), ())), preferred_element_type=jnp.float32)


def tn(a, b):
    return lax.dot_general(a, b, (((0,), (0,)), ((), ())), preferred_element_type=jnp.float32)


def group_slices(width):
    return [slice(g * LANES, (g + 1) * LANES) for g in range(width // LANES)]


def attention_kernel(
    meta_ref,
    query_ref,
    grad_ref,
    held_ref,
    pos_ref,
    attended_ref,
    grad_query_ref,
    own_ref,
    back_ref,
    queries,
    grads,
    self_keys,
    self_values,
    weights,
    self_weights,
    row_max,
    row_sum,
    summed,
    delta,
    *,
    rows,
    tile,
    tiles,
    rim,
    start_pos,
):
    total = rows * GROUP
    window = rows * (rim + 1)
    my_index = meta_ref[0]
    base = my_index * rows
    heads = [slice(h * rows, (h + 1) * rows) for h in range(GROUP)]
    cols = [slice(h * HD, (h + 1) * HD) for h in range(GROUP)]
    lanes = group_slices(tile)
    self_lanes = group_slices(window)
    for h in range(GROUP):
        queries[heads[h], :] = query_ref[:, cols[h]]
        grads[heads[h], :] = grad_ref[:, cols[h]]
    for d in range(rim + 1):
        owner = jnp.maximum(my_index - rim + d, 0)
        block = slice(d * rows, (d + 1) * rows)
        self_keys[block, :] = held_ref[owner, tile : tile + rows, :HD]
        self_values[block, :] = held_ref[owner, tile : tile + rows, HD:]

    row = lax.broadcasted_iota(jnp.int32, (rows, LANES), 0)
    lane = lax.broadcasted_iota(jnp.int32, (rows, LANES), 1)
    bound = start_pos + jnp.maximum(base + row - (WINDOW - 1), 0)
    first = window - rows
    self_scores = nt(queries[...], self_keys[...])
    for hs in heads:
        best = None
        for g, ls in enumerate(self_lanes):
            key = lane + g * LANES
            visible = (
                (key <= row + first) & (key >= row + (first - WINDOW + 1)) & (key >= first - base)
            )
            masked = jnp.where(visible, self_scores[hs, ls], NEG)
            self_weights[hs, ls] = masked
            best = masked if best is None else jnp.maximum(best, masked)
        row_max[hs, :] = best

    def score_pass(t, carry):
        scores = nt(queries[...], held_ref[t, :tile, :HD])
        for hs in heads:
            best = row_max[hs, :]
            for ls in lanes:
                masked = jnp.where(pos_ref[t, :, ls] < bound, scores[hs, ls], NEG)
                weights[t, hs, ls] = masked
                best = jnp.maximum(best, masked)
            row_max[hs, :] = best
        return carry

    lax.fori_loop(0, tiles, score_pass, 0)
    row_max[...] = jnp.broadcast_to(
        jnp.max(row_max[...], axis=1, keepdims=True), (total, LANES)
    )

    for hs in heads:
        best = row_max[hs, :]
        added = jnp.zeros((rows, LANES), jnp.float32)
        for ls in self_lanes:
            part = jnp.exp2((self_weights[hs, ls] - best) * EXP2_SCALE)
            self_weights[hs, ls] = part
            added = added + part
        row_sum[hs, :] = added

    def exp_pass(t, carry):
        for hs in heads:
            best = row_max[hs, :]
            added = row_sum[hs, :]
            for ls in lanes:
                part = jnp.exp2((weights[t, hs, ls] - best) * EXP2_SCALE)
                weights[t, hs, ls] = part
                added = added + part
            row_sum[hs, :] = added
        return carry

    lax.fori_loop(0, tiles, exp_pass, 0)
    row_sum[...] = jnp.broadcast_to(
        1.0 / jnp.sum(row_sum[...], axis=1, keepdims=True), (total, LANES)
    )

    def normalised(ref, index, groups):
        parts = []
        for hs in heads:
            inverse = row_sum[hs, :]
            pieces = []
            for ls in groups:
                weight = ref[(*index, hs, ls)] * inverse
                ref[(*index, hs, ls)] = weight
                pieces.append(weight.astype(jnp.bfloat16))
            parts.append(jnp.concatenate(pieces, axis=1))
        return jnp.concatenate(parts, axis=0)

    rounded = normalised(self_weights, (), self_lanes)
    summed[...] = nn(rounded, self_values[...])
    value_grads = tn(rounded, grads[...])
    own_ref[:, HD:] = value_grads[first:, :]
    back_ref[:, HD:] = value_grads[:first, :].astype(jnp.bfloat16)

    def value_pass(t, carry):
        rounded = normalised(weights, (t,), lanes)
        summed[...] += nn(rounded, held_ref[t, :tile, HD:])
        return carry

    lax.fori_loop(0, tiles, value_pass, 0)
    for hs, cs in zip(heads, cols):
        out = summed[hs, :].astype(jnp.bfloat16)
        attended_ref[:, cs] = out
        products = out.astype(jnp.float32) * grads[hs, :].astype(jnp.float32)
        delta[hs, :] = jnp.broadcast_to(jnp.sum(products, axis=1, keepdims=True), (rows, LANES))

    def score_grads(grad_weights, ref, index, groups):
        parts = []
        for hs in heads:
            shift = delta[hs, :]
            pieces = [
                (ref[(*index, hs, ls)] * (grad_weights[hs, ls] - shift)).astype(jnp.bfloat16)
                for ls in groups
            ]
            parts.append(jnp.concatenate(pieces, axis=1))
        return jnp.concatenate(parts, axis=0)

    grad_scores = score_grads(nt(grads[...], self_values[...]), self_weights, (), self_lanes)
    summed[...] = nn(grad_scores, self_keys[...])
    key_grads = tn(grad_scores, queries[...])
    own_ref[:, :HD] = key_grads[first:, :]
    back_ref[:, :HD] = key_grads[:first, :].astype(jnp.bfloat16)

    def grad_pass(t, carry):
        grad_weights = nt(grads[...], held_ref[t, :tile, HD:])
        grad_scores = score_grads(grad_weights, weights, (t,), lanes)
        summed[...] += nn(grad_scores, held_ref[t, :tile, :HD])
        return carry

    lax.fori_loop(0, tiles, grad_pass, 0)
    for hs, cs in zip(heads, cols):
        grad_query_ref[:, cs] = (summed[hs, :] * SCALE).astype(jnp.bfloat16)


def attention(my_index, query, d_out, held, positions, start_pos):
    rows = query.shape[0]
    tiles, tile = positions.shape
    rim = (WINDOW + rows - 2) // rows
    window = rows * (rim + 1)
    total = rows * GROUP
    whole = pl.BlockSpec(memory_space=pltpu.VMEM)
    return pl.pallas_call(
        functools.partial(
            attention_kernel, rows=rows, tile=tile, tiles=tiles, rim=rim, start_pos=start_pos
        ),
        in_specs=[pl.BlockSpec(memory_space=pltpu.SMEM)] + [whole] * 4,
        out_specs=[whole] * 4,
        out_shape=[
            jax.ShapeDtypeStruct((rows, GROUP * HD), jnp.bfloat16),
            jax.ShapeDtypeStruct((rows, GROUP * HD), jnp.bfloat16),
            jax.ShapeDtypeStruct((rows, 2 * HD), jnp.float32),
            jax.ShapeDtypeStruct((window - rows, 2 * HD), jnp.bfloat16),
        ],
        scratch_shapes=[
            pltpu.VMEM((total, HD), jnp.bfloat16),
            pltpu.VMEM((total, HD), jnp.bfloat16),
            pltpu.VMEM((window, HD), jnp.bfloat16),
            pltpu.VMEM((window, HD), jnp.bfloat16),
            pltpu.VMEM((tiles, total, tile), jnp.float32),
            pltpu.VMEM((total, window), jnp.float32),
            pltpu.VMEM((total, LANES), jnp.float32),
            pltpu.VMEM((total, LANES), jnp.float32),
            pltpu.VMEM((total, HD), jnp.float32),
            pltpu.VMEM((total, LANES), jnp.float32),
        ],
        compiler_params=pltpu.CompilerParams(vmem_limit_bytes=58 * 1024 * 1024),
        name="attention",
    )(my_index, query, d_out, held, positions[:, None, :])


def local(query, self_keys, self_values, cache_keys, cache_values, cache_pos, d_out):
    rows = query.shape[0]
    cache_dev = cache_keys.shape[0]
    peers = lax.axis_size("seq")
    my_index = lax.axis_index("seq")
    start_pos = (cache_dev - rows) * peers
    rim = (WINDOW + rows - 2) // rows
    digits = jnp.concatenate([cache_pos // POS_BASE, cache_pos % POS_BASE]).astype(jnp.bfloat16)
    digit_rows = 2 * cache_dev // (2 * HD)
    digits = jnp.pad(digits.reshape(digit_rows, 2 * HD), ((0, POS_ROWS - digit_rows), (0, 0)))
    sent = jnp.concatenate(
        [
            jnp.concatenate([cache_keys, cache_values], axis=1),
            jnp.concatenate([self_keys, self_values], axis=1),
            digits,
        ],
        axis=0,
    )
    held = lax.all_gather(sent, "seq", axis=0)
    got = held[:, cache_dev + rows : cache_dev + rows + digit_rows, :].astype(jnp.int32)
    got = got.reshape(peers, 2, cache_dev)
    positions = got[:, 0] * POS_BASE + got[:, 1]
    attended, grad_query, own, back = attention(
        my_index.reshape(1), query, d_out, held, positions, start_pos
    )
    total = own
    for distance in range(1, rim + 1):
        block = back[(rim - distance) * rows : (rim - distance + 1) * rows]
        route = [(i, i - distance) for i in range(distance, peers)]
        total = total + lax.ppermute(block, "seq", route).astype(jnp.float32)
    grad_keys = (total[:, :HD] * SCALE).astype(jnp.bfloat16)
    grad_values = total[:, HD:].astype(jnp.bfloat16)
    return attended, grad_query, grad_keys, grad_values


def solution(mesh):
    split = P(("batch", "seq"), "kvh")
    return jax.shard_map(
        local,
        mesh=mesh,
        in_specs=(split,) * 5 + (P(("batch", "seq")), split),
        out_specs=(split,) * 4,
        check_vma=False,
    )
```

time: 201 us -> 110 us (0.55)
  matrix products: 94.9 us -> 0 us
  starting transfers between devices: 46 us -> 11.9 us
  waiting for transfers between devices: 16.8 us -> 46.4 us
  Pallas kernels: 0 us -> 28.6 us
  other arithmetic: 14.5 us -> 5.57 us
  local copies, waits for them, and re-layouts: 9.95 us -> 1.67 us
  loops' own time: 2.63 us -> 0 us
    dot_general x70 -> x0, matrix products: 94.9 us -> none  [the longest x16 26.4 us: forward_piece(): jnp.einsum('gtc,cd->gtd', weights, values, preferred_element_type=jnp.flo...]
    all_gather x1, waiting for transfers between devices: 10.1 us -> 42.6 us  [local(): held = lax.all_gather(sent, 'seq', axis=0)]
    pallas_call x0 -> x1, Pallas kernels: none -> 28.6 us  [attention(): pl.pallas_call(functools.partial(attention_kernel, rows=rows, tile=tile,...]
    ppermute x16 -> x4, starting transfers between devices: 36.6 us -> 11.9 us  [local(): total = total + lax.ppermute(block, 'seq', route).astype(jnp.float32)]
    all_to_all x1 -> x0, starting transfers between devices: 9.37 us -> none  [copy_for_each(): lax.all_to_all(jnp.broadcast_to(value[None], (peers, *value.shape)), axis...]
    lt x48 -> x0, other arithmetic: 6.47 us -> none  [the longest x32 4.31 us: forward_piece(): visible = positions[None, :] < bound_pos[:, None]]
    split x1 -> x0, local copies, waits for them, and re-layouts: 4.47 us -> none  [side_by_side(): jnp.split(out, [sum(widths[:k]) for k in range(1, len(widths))], axis=along)]
    unnamed x21 -> x0, local copies, waits for them, and re-layouts: 3.31 us -> none
  transfers between devices with their start and end apart: 18 -> 5, of which waited for: 4 -> 3; matrix products, arithmetic and copies ran while one was open for 28% -> 0% of each run, Pallas kernels for 0% -> 0%
where the time goes in v1:
time: 110 us; the launch traced here: 108 us
  waiting for transfers between devices  46.4 us (42%)
  Pallas kernels  28.6 us (26%)
  between operations  14.1 us (13%)
  starting transfers between devices  11.9 us (11%)
  other arithmetic  5.57 us (5%)
  local copies, waits for them, and re-layouts  1.67 us (2%)
    all_gather x1, waiting for transfers between devices, local(): held = lax.all_gather(sent, 'seq', axis=0)  42.6 us
    pallas_call x1, Pallas kernels, attention(): pl.pallas_call(functools.partial(attention_kernel, rows=rows, tile=tile,...  28.6 us
    ppermute x4, starting transfers between devices, local(): total = total + lax.ppermute(block, 'seq', route).astype(jnp.float32)  11.9 us
    ppermute x4, waiting for transfers between devices, local(): total = total + lax.ppermute(block, 'seq', route).astype(jnp.float32)  3.79 us
  transfers between devices with their start and end apart: 5, of which 3 were waited for; matrix products, arithmetic and copies ran while one was open for 0% of the time, Pallas kernels for 0%

profile of v1, /device:TPU:194, one launch (start us, length us, event | category | flops | bytes accessed | tf_op | source)
XLA Modules:
  0.0 108.3 jit_solution(642714336514946853)
XLA Ops:
  7.2 0.0 all-gather.3.cloned.1.call-start
  7.2 0.7 fusion.4
  8.0 1.8 %pad_maximum_fusion = bf16[656,256]{1,0:T(8,128)(2,1)} fusion(bf16[16,256]{1,0:T(8,128)(2,1)S(1)} %fusion.3, bf16[128,128]{1,0:T(8,128)(2,1)} %param.9, bf16[128,128]{1,0:T(8,128)(2,1)} %param.8, bf16[512,128]{1,0:T(8,128)(2,1)} %param.11, bf16[512,128]{1,0:T(8,128)(2,1)} %param.10), kind=kLoop, calls=%fused_computation | loop fusion | flops 1679360 | bytes 671744 | tf_op jit(solution)/shard_map/concatenate | solution.py:243
  9.7 0.0 all-gather.3.cloned.1.call-update
  9.8 42.6 %all-gather.3.cloned.1.call-done = bf16[10496,256]{1,0:T(8,128)(2,1)} async-done(((bf16[656,256]{1,0:T(8,128)(2,1)}), bf16[10496,256]{1,0:T(8,128)(2,1)}) %all-gather.3.cloned.1.call-update) | async-done | bytes 5373968 | tf_op jit(solution)/shard_map/all_gather | solution.py:251
  52.4 0.9 slice_convert_fusion.1
  53.3 0.1 reshape.26
  53.3 0.7 slice_add_fusion.pos_ref
  54.0 28.6 %attention.1 = (bf16[128,640]{1,0:T(8,128)(2,1)}, bf16[128,640]{1,0:T(8,128)(2,1)}, f32[128,256]{1,0:T(8,128)}, bf16[512,256]{1,0:T(8,128)(2,1)}) custom-call(s32[1]{0:T(128)} %bitcast.meta_ref, bf16[128,640]{1,0:T(8,128)(2,1)} %query_ref.1, bf16[128,640]{1,0:T(8,128)(2,1)} %grad_ref.1, bf16[16,656,256]{2,1,0:T(8,128)(2,1)} %bitcast.3, ...), custom_call_target="tpu_custom_call" | custom-call | tf_op jit(solution)/shard_map/attention/pallas_call | solution.py:204
  82.6 1.0 fusion.7
  83.5 2.4 %collective-permute-start = (bf16[128,256]{1,0:T(8,128)(2,1)S(1)}, bf16[128,256]{1,0:T(8,128)(2,1)S(1)}, u32[]{:S(2)}, u32[]{:S(2)}) collective-permute-start(bf16[128,256]{1,0:T(8,128)(2,1)S(1)} %get-tuple-element.12), channel_id=1, source_target_pairs={{16,0},{32,16},{48,32},{64,48},{80,64},{96,80},{112,96},{128,112},... | collective-permute-start | bytes 196616 | tf_op jit(solution)/shard_map/ppermute | solution.py:262
  86.0 4.6 %collective-permute-start.3 = (bf16[128,256]{1,0:T(8,128)(2,1)S(1)}, bf16[128,256]{1,0:T(8,128)(2,1)S(1)}, u32[]{:S(2)}, u32[]{:S(2)}) collective-permute-start(bf16[128,256]{1,0:T(8,128)(2,1)S(1)} %get-tuple-element.13), channel_id=1, source_target_pairs={{64,0},{80,16},{96,32},{112,48},{128,64},{144,80},{160,96},{176,11... | collective-permute-start | bytes 196616 | tf_op jit(solution)/shard_map/ppermute | solution.py:262
  90.5 2.1 %collective-permute-start.2 = (bf16[128,256]{1,0:T(8,128)(2,1)S(1)}, bf16[128,256]{1,0:T(8,128)(2,1)S(1)}, u32[]{:S(2)}, u32[]{:S(2)}) collective-permute-start(bf16[128,256]{1,0:T(8,128)(2,1)S(1)} %get-tuple-element.14), channel_id=1, source_target_pairs={{48,0},{64,16},{80,32},{96,48},{112,64},{128,80},{144,96},{160,112... | collective-permute-start | bytes 196616 | tf_op jit(solution)/shard_map/ppermute | solution.py:262
  92.7 2.8 %collective-permute-start.1 = (bf16[128,256]{1,0:T(8,128)(2,1)S(1)}, bf16[128,256]{1,0:T(8,128)(2,1)S(1)}, u32[]{:S(2)}, u32[]{:S(2)}) collective-permute-start(bf16[128,256]{1,0:T(8,128)(2,1)S(1)} %get-tuple-element.15), channel_id=1, source_target_pairs={{32,0},{48,16},{64,32},{80,48},{96,64},{112,80},{128,96},{144,112}... | collective-permute-start | bytes 196616 | tf_op jit(solution)/shard_map/ppermute | solution.py:262
  95.4 0.0 collective-permute-done
  95.4 0.0 collective-permute-done.3
  95.4 1.3 %collective-permute-done.2 = bf16[128,256]{1,0:T(8,128)(2,1)S(1)} collective-permute-done((bf16[128,256]{1,0:T(8,128)(2,1)S(1)}, bf16[128,256]{1,0:T(8,128)(2,1)S(1)}, u32[]{:S(2)}, u32[]{:S(2)}) %collective-permute-start.2) | collective-permute-done | bytes 65568 | tf_op jit(solution)/shard_map/ppermute | solution.py:262
  96.8 2.4 %collective-permute-done.1 = bf16[128,256]{1,0:T(8,128)(2,1)S(1)} collective-permute-done((bf16[128,256]{1,0:T(8,128)(2,1)S(1)}, bf16[128,256]{1,0:T(8,128)(2,1)S(1)}, u32[]{:S(2)}, u32[]{:S(2)}) %collective-permute-start.1) | collective-permute-done | bytes 65568 | tf_op jit(solution)/shard_map/ppermute | solution.py:262
  99.2 0.9 convert_add_fusion
  100.2 0.6 slice.51
  100.8 0.6 fusion
  (3 shorter events, 0.0 us)
Async XLA Ops:
  7.2 45.2 %all-gather.3.cloned.1.call-start = ((), (), s32[]{:S(2)}) async-start(), calls=%async_computation | async-start | bytes 5709824 | tf_op jit(solution)/shard_map/all_gather | solution.py:251
  83.5 11.9 %collective-permute-start = (bf16[128,256]{1,0:T(8,128)(2,1)S(1)}, bf16[128,256]{1,0:T(8,128)(2,1)S(1)}, u32[]{:S(2)}, u32[]{:S(2)}) collective-permute-start(bf16[128,256]{1,0:T(8,128)(2,1)S(1)} %get-tuple-element.12), channel_id=1, source_target_pairs={{16,0},{32,16},{48,32},{64,48},{80,64},{96,80},{112,96},{128,112},... | collective-permute-start | bytes 196616 | tf_op jit(solution)/shard_map/ppermute | solution.py:262
  86.0 9.5 %collective-permute-start.3 = (bf16[128,256]{1,0:T(8,128)(2,1)S(1)}, bf16[128,256]{1,0:T(8,128)(2,1)S(1)}, u32[]{:S(2)}, u32[]{:S(2)}) collective-permute-start(bf16[128,256]{1,0:T(8,128)(2,1)S(1)} %get-tuple-element.13), channel_id=1, source_target_pairs={{64,0},{80,16},{96,32},{112,48},{128,64},{144,80},{160,96},{176,11... | collective-permute-start | bytes 196616 | tf_op jit(solution)/shard_map/ppermute | solution.py:262
  90.5 6.3 %collective-permute-start.2 = (bf16[128,256]{1,0:T(8,128)(2,1)S(1)}, bf16[128,256]{1,0:T(8,128)(2,1)S(1)}, u32[]{:S(2)}, u32[]{:S(2)}) collective-permute-start(bf16[128,256]{1,0:T(8,128)(2,1)S(1)} %get-tuple-element.14), channel_id=1, source_target_pairs={{48,0},{64,16},{80,32},{96,48},{112,64},{128,80},{144,96},{160,112... | collective-permute-start | bytes 196616 | tf_op jit(solution)/shard_map/ppermute | solution.py:262
  92.7 6.6 %collective-permute-start.1 = (bf16[128,256]{1,0:T(8,128)(2,1)S(1)}, bf16[128,256]{1,0:T(8,128)(2,1)S(1)}, u32[]{:S(2)}, u32[]{:S(2)}) collective-permute-start(bf16[128,256]{1,0:T(8,128)(2,1)S(1)} %get-tuple-element.15), channel_id=1, source_target_pairs={{32,0},{48,16},{64,32},{80,48},{96,64},{112,80},{128,96},{144,112}... | collective-permute-start | bytes 196616 | tf_op jit(solution)/shard_map/ppermute | solution.py:262
Sparse Core Ops, SparseCore 0:
  9.9 42.4 all-gather.2
